TPU v7x, 256 devices: a whole 4x4x8 slice. The times are simulated.
256 devices in a mesh: seq: 8 (over x_hi, y), row: 32 (over x_lo, z, core).
Axes of the slice: x: 4 (x_hi: 2, x_lo: 2; x = x_hi * 2 + x_lo), y: 4, z: 8, core: 2. Of those that a mesh axis runs over, the one named last changes fastest.
Arguments:
- tokens: bfloat16 [2, 2048, 3072], P(None, ('seq', 'row')), may hold values from -6 to 6
- w_qkv: bfloat16 [6144, 3072], P('row'), may hold values from -0.109375 to 0.109375
- w_rate: bfloat16 [32, 3072], P('row'), may hold values from -0.109375 to 0.109375
- rate_bias: float32 [32], P('row'), may hold values from -3 to 1
- w_out: bfloat16 [2048, 3072], P('row'), may hold values from -0.125 to 0.125
- w_first_init: float32 [32, 64, 256], P('row'), may hold values from -0.75 to 0.75
- b_first_init: float32 [32, 256], P('row'), may hold values from -3 to 3
- w_second_init: float32 [32, 256, 64], P('row'), may hold values from -0.375 to 0.375
- b_second_init: float32 [32, 64], P('row'), may hold values from -3 to 3
- ln_gain: float32 [32, 64], P('row'), may hold values from 0.5 to 1.5
- ln_bias: float32 [32, 64], P('row'), may hold values from -3 to 3
Outputs:
- mixed: bfloat16 [2, 2048, 3072], P(None, ('seq', 'row'))
All inputs are finite; a program needn't handle non-finite values.
Results may differ from a plain program's by a relative error of at most 0.0056.
Values may be sent and summed in bfloat16 or wider, within the bound.
A program may use at most 64 MiB of HBM per device.

v0:
```python
from functools import partial
import jax
import jax.numpy as jnp
from jax import lax
from jax.sharding import PartitionSpec as P

MINI = 64
gelu_coef = 0.7978845608028654
base_rate = 0.01
ln_eps = 1e-06


def passed_along(array, axis, by):
    size = lax.axis_size(axis)
    pairs = [(i, i + by) for i in range(size) if 0 <= i + by < size]
    return lax.ppermute(array, axis, pairs)


def gelu_tanh(entries):
    tanh_arg = gelu_coef * (entries + 0.044715 * entries * entries * entries)
    return 0.5 * entries * (1.0 + jnp.tanh(tanh_arg))


def gelu_slope(entries):
    tanh_arg = gelu_coef * (entries + 0.044715 * entries * entries * entries)
    tangent = jnp.tanh(tanh_arg)
    return 0.5 * (1.0 + tangent) + 0.5 * entries * (1.0 - tangent * tangent) * gelu_coef * (
        1.0 + 3.0 * 0.044715 * entries * entries
    )


def matmul(left, right):
    return jnp.dot(left, right, precision=lax.Precision.HIGHEST, preferred_element_type=jnp.float32)


def normalize(entries):
    centred = entries - jnp.mean(entries, axis=-1, keepdims=True)
    spread = jnp.sqrt(jnp.mean(centred * centred, axis=-1, keepdims=True) + ln_eps)
    return (centred / spread, spread)


def mini_step(inner_state, batch_block, norm_gain, offset):
    w_first, b_first, w_second, b_second = inner_state
    queries, key_rows, value_rows, lr_rows = batch_block
    mini_len = queries.shape[0]
    hidden_pre = matmul(key_rows, w_first) + b_first
    hidden = gelu_tanh(hidden_pre)
    second = matmul(hidden, w_second) + b_second
    target = value_rows - key_rows
    normed, spread = normalize(second)
    grad_out = norm_gain * (norm_gain * normed + offset - target)
    feat_width = second.shape[-1]
    grad_second = (
        feat_width * grad_out
        - jnp.sum(grad_out, axis=-1, keepdims=True)
        - normed * jnp.sum(grad_out * normed, axis=-1, keepdims=True)
    ) / (feat_width * spread)
    grad_first = matmul(grad_second, w_second.T) * gelu_slope(hidden_pre)
    tri_mask = jnp.tril(jnp.ones((mini_len, mini_len), jnp.float32))
    eta_last = lr_rows / mini_len
    eta_table = tri_mask * eta_last[None, :]
    query_keys = matmul(queries, key_rows.T) * eta_table
    bias_first = b_first - matmul(eta_table, grad_first)
    first_bar = matmul(queries, w_first) - matmul(query_keys, grad_first) + bias_first
    hidden_bar = gelu_tanh(first_bar)
    hidden_pairs = matmul(hidden_bar, hidden.T) * eta_table
    bias_second = b_second - matmul(eta_table, grad_second)
    second_bar = matmul(hidden_bar, w_second) - matmul(hidden_pairs, grad_second) + bias_second
    w_first = w_first - matmul((key_rows * eta_last[:, None]).T, grad_first)
    b_first = b_first - matmul(eta_last[None, :], grad_first)[0]
    w_second = w_second - matmul((hidden * eta_last[:, None]).T, grad_second)
    b_second = b_second - matmul(eta_last[None, :], grad_second)[0]
    normed_bar, spread_bar = normalize(second_bar)
    result = queries + norm_gain * normed_bar + offset
    return ((w_first, b_first, w_second, b_second), result)


def run_blocks(inner_state, queries, key_rows, value_rows, lr_rows, norm_gain, offset, mini_len):
    block_count = queries.shape[0] // mini_len
    blocks = (
        queries.reshape(block_count, mini_len, -1),
        key_rows.reshape(block_count, mini_len, -1),
        value_rows.reshape(block_count, mini_len, -1),
        lr_rows.reshape(block_count, mini_len),
    )

    def advance(loop_carry, batch_block):
        return mini_step(loop_carry, batch_block, norm_gain, offset)

    inner_state, results = lax.scan(advance, inner_state, blocks)
    return (inner_state, results.reshape(queries.shape[0], -1))


def pack_state(state):
    videos = state[0].shape[0]
    return jnp.concatenate([part.reshape(videos, -1) for part in state], axis=1)


def unpack_state(flat, like):
    parts = []
    at = 0
    for part in like:
        width = part[0].size
        parts.append(flat[:, at : at + width].reshape(part.shape))
        at += width
    return tuple(parts)


def on_device(
    tokens,
    w_qkv,
    w_rate,
    rate_bias,
    w_out,
    w_first_init,
    b_first_init,
    w_second_init,
    b_second_init,
    ln_gain,
    ln_bias,
):
    videos, tok_part, feat_width = tokens.shape
    row_axes = ("xlo", "z", "core")
    pair_axes = ("xlo", "core")
    row_count = lax.axis_size(row_axes)
    z_count = lax.axis_size("z")
    pair_count = lax.axis_size(pair_axes)
    seg_len = tok_part * row_count
    proj_width = w_qkv.shape[0]
    head_size = proj_width // 3
    stacked = jnp.concatenate([w_qkv, w_rate], axis=0)
    gathered = lax.all_gather(tokens, row_axes, axis=1, tiled=True)
    gathered, w_out = lax.optimization_barrier((gathered, w_out))
    w_out_pair = lax.all_gather(w_out, pair_axes, axis=0, tiled=True)
    combined = jnp.einsum("vkd,cd->vkc", gathered, stacked, preferred_element_type=jnp.float32)
    projected = lax.optimization_barrier(combined[:, :, :proj_width].astype(jnp.bfloat16)).astype(
        jnp.float32
    )
    queries = projected[:, :, :head_size]
    key_rows = projected[:, :, head_size : 2 * head_size]
    value_rows = projected[:, :, 2 * head_size :]
    lr_rows = base_rate * jax.nn.sigmoid(combined[:, :, proj_width] + rate_bias[0])
    initial = (w_first_init[0], b_first_init[0], w_second_init[0], b_second_init[0])
    norm_gain = ln_gain[0]
    offset = ln_bias[0]

    def segment(inner_state, video_q, video_k, video_v, video_lr):
        return run_blocks(inner_state, video_q, video_k, video_v, video_lr, norm_gain, offset, MINI)

    seq_count = lax.axis_size("seq")
    seq_place = lax.axis_index("seq")
    first_device = seq_place == 0

    def spread_videos(entries):
        return jnp.broadcast_to(entries, (videos,) + entries.shape)

    start_states = jax.tree.map(spread_videos, initial)
    incoming = start_states
    for turn_idx in range(seq_count):
        finals, results = jax.vmap(segment)(incoming, queries, key_rows, value_rows, lr_rows)
        if turn_idx == 1:
            w_out_pair, finals = lax.optimization_barrier((w_out_pair, finals))
        if turn_idx + 1 < seq_count:
            with jax.named_scope("state_hop"):
                received = unpack_state(passed_along(pack_state(finals), "seq", 1), finals)
            incoming = jax.tree.map(partial(jnp.where, first_device), start_states, received)
    heads_rows = results.astype(jnp.bfloat16)
    with jax.named_scope("output_mix"):
        by_owner = heads_rows.reshape(videos, 2, z_count, 2, tok_part, head_size)
        by_owner = by_owner.transpose(1, 3, 0, 2, 4, 5).reshape(
            pair_count, videos, z_count, tok_part, head_size
        )
        by_head = lax.all_to_all(by_owner, pair_axes, 0, 0, tiled=True)
        partial_terms = jnp.einsum(
            "gvzic,gcd->zvid",
            by_head,
            w_out_pair.reshape(pair_count, head_size, feat_width),
            preferred_element_type=jnp.float32,
        )
        pieces = lax.all_to_all(partial_terms, "z", 0, 0, tiled=True)
        mixed_out = jnp.sum(pieces, axis=0)
    return mixed_out.reshape(videos, tok_part, feat_width).astype(jnp.bfloat16)


def solution(mesh):
    seq_count, row_count = mesh.devices.shape
    fine = jax.sharding.Mesh(
        mesh.devices.reshape(seq_count, 2, row_count // 4, 2), ("seq", "xlo", "z", "core")
    )
    row = ("xlo", "z", "core")
    in_specs = (
        P(None, ("seq",) + row, None),
        P(row, None),
        P(row, None),
        P(row),
        P(row, None),
        P(row, None, None),
        P(row, None),
        P(row, None, None),
        P(row, None),
        P(row, None),
        P(row, None),
    )
    out_specs = P(None, ("seq",) + row, None)
    return jax.shard_map(
        on_device, mesh=fine, in_specs=in_specs, out_specs=out_specs, check_vma=False
    )
```

profile of v0, /device:TPU:4, one launch (start us, length us, event | category | flops | bytes accessed | tf_op | source)
XLA Modules:
  0.0 341.9 jit_solution(8566038847159366962)
XLA Ops:
  7.9 70.0 %all-gather.3.cloned.1.call-done = bf16[2,256,3072]{2,1,0:T(8,128)(2,1)} async-done(((bf16[2,8,3072]{2,1,0:T(8,128)(2,1)}), bf16[2,256,3072]{2,1,0:T(8,128)(2,1)}) %all-gather.3.cloned.1.call-update) | async-done | bytes 3145744 | tf_op jit(solution)/shard_map/all_gather | solution.py:132
  78.0 3.4 fusion.200
  82.3 10.8 %while.130 = (s32[]{:T(128)}, f32[2,64,256]{2,1,0:T(8,128)S(1)}, f32[2,256]{1,0:T(2,128)S(1)}, f32[2,256,64]{1,2,0:T(8,128)S(1)}, f32[2,64]{1,0:T(2,128)S(1)}, /...) while((s32[]{:T(128)}, f32[2,64,256]{2,1,0:T(8,128)S(1)}, ...), condition=%wide.region_5.6_spmd, body=%wide.region_0.5_spmd.sunk | while | flops 127755136 | bytes 2386049 | solution.py:90
  93.7 3.4 collective-permute-start
  97.2 10.5 %collective-permute-done = f32[2,33088]{1,0:T(2,128)S(1)} collective-permute-done((f32[2,33088]{1,0:T(2,128)S(1)}, f32[2,33088]{1,0:T(2,128)S(1)}, u32[]{:S(2)}, u32[]{:S(2)}) %collective-permute-start) | collective-permute-done | bytes 264736 | tf_op jit(solution)/shard_map/state_hop/ppermute | solution.py:16
  108.1 10.8 %while.131 = (s32[]{:T(128)}, f32[2,64,256]{2,1,0:T(8,128)S(1)}, f32[2,256]{1,0:T(2,128)S(1)}, f32[2,256,64]{1,2,0:T(8,128)S(1)}, f32[2,64]{1,0:T(2,128)S(1)}, /...) while((s32[]{:T(128)}, f32[2,64,256]{2,1,0:T(8,128)S(1)}, ...), condition=%wide.region_11.12_spmd, body=%wide.region_6.11_spmd.sunk | while | flops 127755136 | bytes 2386049 | solution.py:90
  118.9 5.2 %all-gather.5.cloned.1.call-done = bf16[256,3072]{1,0:T(8,128)(2,1)} async-done(((bf16[64,3072]{1,0:T(8,128)(2,1)}), bf16[256,3072]{1,0:T(8,128)(2,1)}) %all-gather.5.cloned.1.call-update) | async-done | bytes 1572880 | tf_op jit(solution)/shard_map/all_gather | solution.py:134
  124.7 3.3 collective-permute-start.1
  128.0 10.7 %collective-permute-done.1 = f32[2,33088]{1,0:T(2,128)S(1)} collective-permute-done((f32[2,33088]{1,0:T(2,128)S(1)}, f32[2,33088]{1,0:T(2,128)S(1)}, u32[]{:S(2)}, u32[]{:S(2)}) %collective-permute-start.1) | collective-permute-done | bytes 264736 | tf_op jit(solution)/shard_map/state_hop/ppermute | solution.py:16
  139.2 10.8 %while.132 = (s32[]{:T(128)}, f32[2,64,256]{2,1,0:T(8,128)S(1)}, f32[2,256]{1,0:T(2,128)S(1)}, f32[2,256,64]{1,2,0:T(8,128)S(1)}, f32[2,64]{1,0:T(2,128)S(1)}, /...) while((s32[]{:T(128)}, f32[2,64,256]{2,1,0:T(8,128)S(1)}, ...), condition=%wide.region_17.18_spmd, body=%wide.region_12.17_spmd.sunk | while | flops 127755136 | bytes 2386049 | solution.py:90
  152.5 11.4 %collective-permute-done.2 = f32[2,33088]{1,0:T(2,128)S(1)} collective-permute-done((f32[2,33088]{1,0:T(2,128)S(1)}, f32[2,33088]{1,0:T(2,128)S(1)}, u32[]{:S(2)}, u32[]{:S(2)}) %collective-permute-start.2) | collective-permute-done | bytes 264736 | tf_op jit(solution)/shard_map/state_hop/ppermute | solution.py:16
  164.2 10.8 %while.133 = (s32[]{:T(128)}, f32[2,64,256]{2,1,0:T(8,128)S(1)}, f32[2,256]{1,0:T(2,128)S(1)}, f32[2,256,64]{1,2,0:T(8,128)S(1)}, f32[2,64]{1,0:T(2,128)S(1)}, /...) while((s32[]{:T(128)}, f32[2,64,256]{2,1,0:T(8,128)S(1)}, ...), condition=%wide.region_23.24_spmd, body=%wide.region_18.23_spmd.sunk | while | flops 127755136 | bytes 2386049 | solution.py:90
  175.6 2.1 collective-permute-start.3
  177.7 10.3 %collective-permute-done.3 = f32[2,33088]{1,0:T(2,128)S(1)} collective-permute-done((f32[2,33088]{1,0:T(2,128)S(1)}, f32[2,33088]{1,0:T(2,128)S(1)}, u32[]{:S(2)}, u32[]{:S(2)}) %collective-permute-start.3) | collective-permute-done | bytes 264736 | tf_op jit(solution)/shard_map/state_hop/ppermute | solution.py:16
  188.4 10.8 %while.134 = (s32[]{:T(128)}, f32[2,64,256]{2,1,0:T(8,128)S(1)}, f32[2,256]{1,0:T(2,128)S(1)}, f32[2,256,64]{1,2,0:T(8,128)S(1)}, f32[2,64]{1,0:T(2,128)S(1)}, /...) while((s32[]{:T(128)}, f32[2,64,256]{2,1,0:T(8,128)S(1)}, ...), condition=%wide.region_29.30_spmd, body=%wide.region_24.29_spmd.sunk | while | flops 127755136 | bytes 2386049 | solution.py:90
  199.7 1.9 collective-permute-start.4
  201.6 10.0 %collective-permute-done.4 = f32[2,33088]{1,0:T(2,128)S(1)} collective-permute-done((f32[2,33088]{1,0:T(2,128)S(1)}, f32[2,33088]{1,0:T(2,128)S(1)}, u32[]{:S(2)}, u32[]{:S(2)}) %collective-permute-start.4) | collective-permute-done | bytes 264736 | tf_op jit(solution)/shard_map/state_hop/ppermute | solution.py:16
  212.0 10.8 %while.135 = (s32[]{:T(128)}, f32[2,64,256]{2,1,0:T(8,128)S(1)}, f32[2,256]{1,0:T(2,128)S(1)}, f32[2,256,64]{1,2,0:T(8,128)S(1)}, f32[2,64]{1,0:T(2,128)S(1)}, /...) while((s32[]{:T(128)}, f32[2,64,256]{2,1,0:T(8,128)S(1)}, ...), condition=%wide.region_35.36_spmd, body=%wide.region_30.35_spmd.sunk | while | flops 127755136 | bytes 2386049 | solution.py:90
  225.3 10.0 %collective-permute-done.5 = f32[2,33088]{1,0:T(2,128)S(1)} collective-permute-done((f32[2,33088]{1,0:T(2,128)S(1)}, f32[2,33088]{1,0:T(2,128)S(1)}, u32[]{:S(2)}, u32[]{:S(2)}) %collective-permute-start.5) | collective-permute-done | bytes 264736 | tf_op jit(solution)/shard_map/state_hop/ppermute | solution.py:16
  235.7 10.8 %while.136 = (s32[]{:T(128)}, f32[2,64,256]{2,1,0:T(8,128)S(1)}, f32[2,256]{1,0:T(2,128)S(1)}, f32[2,256,64]{1,2,0:T(8,128)S(1)}, f32[2,64]{1,0:T(2,128)S(1)}, /...) while((s32[]{:T(128)}, f32[2,64,256]{2,1,0:T(8,128)S(1)}, ...), condition=%wide.region_41.42_spmd, body=%wide.region_36.41_spmd.sunk | while | flops 127755136 | bytes 2386049 | solution.py:90
  249.3 9.7 %collective-permute-done.6 = f32[2,33088]{1,0:T(2,128)S(1)} collective-permute-done((f32[2,33088]{1,0:T(2,128)S(1)}, f32[2,33088]{1,0:T(2,128)S(1)}, u32[]{:S(2)}, u32[]{:S(2)}) %collective-permute-start.6) | collective-permute-done | bytes 264736 | tf_op jit(solution)/shard_map/state_hop/ppermute | solution.py:16
  259.4 20.8 %while.137 = (s32[]{:T(128)}, f32[2,64,256]{2,1,0:T(8,128)S(1)}, f32[2,256]{1,0:T(2,128)S(1)}, f32[2,256,64]{1,2,0:T(8,128)S(1)}, f32[2,64]{1,0:T(2,128)S(1)}, /...) while((s32[]{:T(128)}, f32[2,64,256]{2,1,0:T(8,128)S(1)}, ...), condition=%wide.region_49.50_spmd, body=%wide.region_42.49_spmd.sunk | while | flops 273236992 | bytes 4856473 | solution.py:90
  280.4 6.5 %all_to_all.10 = bf16[4,2,4096]{2,1,0:T(2,128)(2,1)S(1)} all-to-all(bf16[4,2,4096]{2,1,0:T(2,128)(2,1)S(1)} %reshape.525), channel_id=1, replica_groups=mesh['seq'=8,'xlo'=2,'z'=8,'core'=2] {'xlo','core'}, dimensions={0} | all-to-all | bytes 131072 | tf_op jit(solution)/shard_map/output_mix/all_to_all | solution.py:173
  287.6 46.7 %all_to_all.11 = f32[8,2,8,3072]{3,2,1,0:T(8,128)S(1)} all-to-all(f32[8,2,8,3072]{3,2,1,0:T(8,128)S(1)} %copy.214), channel_id=1, replica_groups=mesh['seq'=8,'xlo'=2,'z'=8,'core'=2] {'z'}, dimensions={0} | all-to-all | bytes 3145728 | tf_op jit(solution)/shard_map/output_mix/all_to_all | solution.py:180
  (685 shorter events, 109.4 us)
Async XLA Ops:
  6.5 71.4 %all-gather.3.cloned.1.call-start = ((), (), s32[]{:S(2)}) async-start(), calls=%async_computation.2 | async-start | bytes 3244032 | tf_op jit(solution)/shard_map/all_gather | solution.py:132
  7.3 116.9 %all-gather.5.cloned.1.call-start = ((), (), s32[]{:S(2)}) async-start(), calls=%async_computation.3 | async-start | bytes 1966080 | tf_op jit(solution)/shard_map/all_gather | solution.py:134
  81.4 0.9 copy-start
  81.4 0.9 copy-start.4
  81.4 0.9 copy-start.5
  81.4 0.9 copy-start.3
  81.4 0.9 copy-start.1
  81.4 0.9 copy-start.2
  93.7 14.0 %collective-permute-start = (f32[2,33088]{1,0:T(2,128)S(1)}, f32[2,33088]{1,0:T(2,128)S(1)}, u32[]{:S(2)}, u32[]{:S(2)}) collective-permute-start(f32[2,33088]{1,0:T(2,128)S(1)} %pad_maximum_fusion), channel_id=1, source_target_pairs={{0,32},{32,64},{64,96},{96,128},{128,160},{160,192},{192,224},{1,3... | collective-permute-start | bytes 794120 | tf_op jit(solution)/shard_map/state_hop/ppermute | solution.py:16
  124.7 14.1 %collective-permute-start.1 = (f32[2,33088]{1,0:T(2,128)S(1)}, f32[2,33088]{1,0:T(2,128)S(1)}, u32[]{:S(2)}, u32[]{:S(2)}) collective-permute-start(f32[2,33088]{1,0:T(2,128)S(1)} %pad_maximum_fusion.1), channel_id=1, source_target_pairs={{0,32},{32,64},{64,96},{96,128},{128,160},{160,192},{192,224},{1,3... | collective-permute-start | bytes 794120 | tf_op jit(solution)/shard_map/state_hop/ppermute | solution.py:16
  150.5 13.3 %collective-permute-start.2 = (f32[2,33088]{1,0:T(2,128)S(1)}, f32[2,33088]{1,0:T(2,128)S(1)}, u32[]{:S(2)}, u32[]{:S(2)}) collective-permute-start(f32[2,33088]{1,0:T(2,128)S(1)} %pad_maximum_fusion.2), channel_id=1, source_target_pairs={{0,32},{32,64},{64,96},{96,128},{128,160},{160,192},{192,224},{1,3... | collective-permute-start | bytes 794120 | tf_op jit(solution)/shard_map/state_hop/ppermute | solution.py:16
  175.6 12.4 %collective-permute-start.3 = (f32[2,33088]{1,0:T(2,128)S(1)}, f32[2,33088]{1,0:T(2,128)S(1)}, u32[]{:S(2)}, u32[]{:S(2)}) collective-permute-start(f32[2,33088]{1,0:T(2,128)S(1)} %pad_maximum_fusion.3), channel_id=1, source_target_pairs={{0,32},{32,64},{64,96},{96,128},{128,160},{160,192},{192,224},{1,3... | collective-permute-start | bytes 794120 | tf_op jit(solution)/shard_map/state_hop/ppermute | solution.py:16
  199.7 11.9 %collective-permute-start.4 = (f32[2,33088]{1,0:T(2,128)S(1)}, f32[2,33088]{1,0:T(2,128)S(1)}, u32[]{:S(2)}, u32[]{:S(2)}) collective-permute-start(f32[2,33088]{1,0:T(2,128)S(1)} %pad_maximum_fusion.4), channel_id=1, source_target_pairs={{0,32},{32,64},{64,96},{96,128},{128,160},{160,192},{192,224},{1,3... | collective-permute-start | bytes 794120 | tf_op jit(solution)/shard_map/state_hop/ppermute | solution.py:16
  223.4 11.9 %collective-permute-start.5 = (f32[2,33088]{1,0:T(2,128)S(1)}, f32[2,33088]{1,0:T(2,128)S(1)}, u32[]{:S(2)}, u32[]{:S(2)}) collective-permute-start(f32[2,33088]{1,0:T(2,128)S(1)} %pad_maximum_fusion.5), channel_id=1, source_target_pairs={{0,32},{32,64},{64,96},{96,128},{128,160},{160,192},{192,224},{1,3... | collective-permute-start | bytes 794120 | tf_op jit(solution)/shard_map/state_hop/ppermute | solution.py:16
  247.1 11.9 %collective-permute-start.6 = (f32[2,33088]{1,0:T(2,128)S(1)}, f32[2,33088]{1,0:T(2,128)S(1)}, u32[]{:S(2)}, u32[]{:S(2)}) collective-permute-start(f32[2,33088]{1,0:T(2,128)S(1)} %pad_maximum_fusion.6), channel_id=1, source_target_pairs={{0,32},{32,64},{64,96},{96,128},{128,160},{160,192},{192,224},{1,3... | collective-permute-start | bytes 794120 | tf_op jit(solution)/shard_map/state_hop/ppermute | solution.py:16
  259.4 27.6 %copy-start.6 = (bf16[256,3072]{1,0:T(8,128)(2,1)S(1)}, bf16[256,3072]{1,0:T(8,128)(2,1)}, u32[]{:S(2)}) copy-start(bf16[256,3072]{1,0:T(8,128)(2,1)} %all-gather.5.cloned.1.call-done) | copy-start | bytes 4718596
Sparse Core Ops, SparseCore 0:
  9.2 68.7 all-gather.2
  97.3 26.7 all-gather.4
where the time goes:
time: 342 us
  waiting for transfers between devices  148 us (43%)
  matrix products  77.1 us (23%)
  blocking collectives  53.2 us (16%)
  other arithmetic  22.5 us (7%)
  starting transfers between devices  16.6 us (5%)
  between operations  14.9 us (4%)
  local copies, waits for them, and re-layouts  6.66 us (2%)
    dot_general x256, matrix products, matmul(): jnp.dot(left, right, precision=lax.Precision.HIGHEST, preferred_element_t...  73.3 us
    ppermute x7, waiting for transfers between devices, passed_along(): return lax.ppermute(array, axis, pairs)  72.5 us
    all_gather x1, waiting for transfers between devices, on_device(): gathered = lax.all_gather(tokens, row_axes, axis=1, tiled=True)  70 us
    all_to_all x1, blocking collectives, on_device(): pieces = lax.all_to_all(partial_terms, 'z', 0, 0, tiled=True)  46.7 us
    ppermute x7, starting transfers between devices, passed_along(): return lax.ppermute(array, axis, pairs)  16.5 us
    reduce_sum x32, other arithmetic, mini_step(): jnp.sum(grad_out, axis=-1, keepdims=True)  6.92 us
  transfers between devices with their start and end apart: 9, of which 9 were waited for; matrix products, arithmetic and copies ran while one was open for 3% of the time, Pallas kernels for 0%

commit v1 on v0

--- a/solution.py
+++ b/solution.py
@@ -129,7 +129,16 @@
     proj_width = w_qkv.shape[0]
     head_size = proj_width // 3
     stacked = jnp.concatenate([w_qkv, w_rate], axis=0)
-    gathered = lax.all_gather(tokens, row_axes, axis=1, tiled=True)
+    test_vectors_up = lambda t0, chip_axis: jnp.concatenate(
+        lax.all_to_all(
+            jnp.stack(lax.axis_size(chip_axis) * [t0]),
+            axis_name=chip_axis,
+            split_axis=0,
+            concat_axis=0,
+        ),
+        axis=1,
+    )
+    gathered = test_vectors_up(tokens, row_axes)
     gathered, w_out = lax.optimization_barrier((gathered, w_out))
     w_out_pair = lax.all_gather(w_out, pair_axes, axis=0, tiled=True)
     combined = jnp.einsum("vkd,cd->vkc", gathered, stacked, preferred_element_type=jnp.float32)

time: 342 us -> 356 us (1.041)
  starting transfers between devices: 16.6 us -> 26.6 us
  local copies, waits for them, and re-layouts: 6.66 us -> 10.8 us
    all_to_all x0 -> x1, waiting for transfers between devices: none -> 72.1 us  [on_device(): lax.all_to_all(jnp.stack(lax.axis_size(chip_axis) * [t0]), axis_name=chip...]
    all_gather x1 -> x0, waiting for transfers between devices: 70 us -> none  [on_device(): gathered = lax.all_gather(tokens, row_axes, axis=1, tiled=True)]
    all_to_all x0 -> x1, starting transfers between devices: none -> 9.49 us  [on_device(): lax.all_to_all(jnp.stack(lax.axis_size(chip_axis) * [t0]), axis_name=chip...]
where the time goes in v1:
time: 356 us
  waiting for transfers between devices  149 us (42%)
  matrix products  76.3 us (21%)
  blocking collectives  53.2 us (15%)
  starting transfers between devices  26.6 us (7%)
  other arithmetic  22.4 us (6%)
  between operations  14.9 us (4%)
  local copies, waits for them, and re-layouts  10.8 us (3%)
    dot_general x256, matrix products, matmul(): jnp.dot(left, right, precision=lax.Precision.HIGHEST, preferred_element_t...  73.3 us
    all_to_all x1, waiting for transfers between devices, on_device(): lax.all_to_all(jnp.stack(lax.axis_size(chip_axis) * [t0]), axis_name=chip...  72.1 us
    ppermute x7, waiting for transfers between devices, passed_along(): return lax.ppermute(array, axis, pairs)  71.2 us
    all_to_all x1, blocking collectives, on_device(): pieces = lax.all_to_all(partial_terms, 'z', 0, 0, tiled=True)  46.7 us
    ppermute x7, starting transfers between devices, passed_along(): return lax.ppermute(array, axis, pairs)  17.1 us
    all_to_all x1, starting transfers between devices, on_device(): lax.all_to_all(jnp.stack(lax.axis_size(chip_axis) * [t0]), axis_name=chip...  9.49 us
  transfers between devices with their start and end apart: 9, of which 9 were waited for; matrix products, arithmetic and copies ran while one was open for 3% of the time, Pallas kernels for 0%

profile of v1, /device:TPU:4, one launch (start us, length us, event | category | flops | bytes accessed | tf_op | source)
XLA Modules:
  0.0 355.5 jit_solution(7537193446403550508)
XLA Ops:
  6.5 2.9 stack.2
  9.5 9.5 %all-to-all-start = ((bf16[32,2,8,3072]{3,2,1,0:T(8,128)(2,1)}), bf16[32,2,8,3072]{3,2,1,0:T(8,128)(2,1)S(1)}, u32[]{:S(2)}, u32[]{:S(2)}) async-start(bf16[32,2,8,3072]{3,2,1,0:T(8,128)(2,1)} %stack.2), calls=%async_computation | async-start | bytes 6291456 | tf_op jit(solution)/shard_map/all_to_all | solution.py:133
  19.7 72.1 %all-to-all-done = bf16[32,2,8,3072]{3,2,1,0:T(8,128)(2,1)S(1)} async-done(((bf16[32,2,8,3072]{3,2,1,0:T(8,128)(2,1)}), bf16[32,2,8,3072]{3,2,1,0:T(8,128)(2,1)S(1)}, u32[]{:S(2)}, u32[]{:S(2)}) %all-to-all-start) | async-done | bytes 3145760 | tf_op jit(solution)/shard_map/all_to_all | solution.py:133
  95.2 10.8 %while.130 = (s32[]{:T(128)}, f32[2,64,256]{2,1,0:T(8,128)S(1)}, f32[2,256]{1,0:T(2,128)S(1)}, f32[2,256,64]{1,2,0:T(8,128)S(1)}, f32[2,64]{1,0:T(2,128)S(1)}, /...) while((s32[]{:T(128)}, f32[2,64,256]{2,1,0:T(8,128)S(1)}, ...), condition=%wide.region_5.6_spmd, body=%wide.region_0.5_spmd.sunk | while | flops 127755136 | bytes 2386049 | solution.py:90
  106.5 3.5 collective-permute-start
  110.2 9.8 %collective-permute-done = f32[2,33088]{1,0:T(2,128)S(1)} collective-permute-done((f32[2,33088]{1,0:T(2,128)S(1)}, f32[2,33088]{1,0:T(2,128)S(1)}, u32[]{:S(2)}, u32[]{:S(2)}) %collective-permute-start) | collective-permute-done | bytes 264736 | tf_op jit(solution)/shard_map/state_hop/ppermute | solution.py:16
  120.3 10.8 %while.131 = (s32[]{:T(128)}, f32[2,64,256]{2,1,0:T(8,128)S(1)}, f32[2,256]{1,0:T(2,128)S(1)}, f32[2,256,64]{1,2,0:T(8,128)S(1)}, f32[2,64]{1,0:T(2,128)S(1)}, /...) while((s32[]{:T(128)}, f32[2,64,256]{2,1,0:T(8,128)S(1)}, ...), condition=%wide.region_11.12_spmd, body=%wide.region_6.11_spmd.sunk | while | flops 127755136 | bytes 2386049 | solution.py:90
  131.1 5.3 %all-gather.2.cloned.1.call-done = bf16[256,3072]{1,0:T(8,128)(2,1)} async-done(((bf16[64,3072]{1,0:T(8,128)(2,1)}), bf16[256,3072]{1,0:T(8,128)(2,1)}) %all-gather.2.cloned.1.call-update) | async-done | bytes 1572880 | tf_op jit(solution)/shard_map/all_gather | solution.py:143
  137.0 3.6 %collective-permute-start.1 = (f32[2,33088]{1,0:T(2,128)S(1)}, f32[2,33088]{1,0:T(2,128)S(1)}, u32[]{:S(2)}, u32[]{:S(2)}) collective-permute-start(f32[2,33088]{1,0:T(2,128)S(1)} %pad_maximum_fusion.1), channel_id=1, source_target_pairs={{0,32},{32,64},{64,96},{96,128},{128,160},{160,192},{192,224},{1,3... | collective-permute-start | bytes 794120 | tf_op jit(solution)/shard_map/state_hop/ppermute | solution.py:16
  140.6 10.5 %collective-permute-done.1 = f32[2,33088]{1,0:T(2,128)S(1)} collective-permute-done((f32[2,33088]{1,0:T(2,128)S(1)}, f32[2,33088]{1,0:T(2,128)S(1)}, u32[]{:S(2)}, u32[]{:S(2)}) %collective-permute-start.1) | collective-permute-done | bytes 264736 | tf_op jit(solution)/shard_map/state_hop/ppermute | solution.py:16
  151.5 10.8 %while.132 = (s32[]{:T(128)}, f32[2,64,256]{2,1,0:T(8,128)S(1)}, f32[2,256]{1,0:T(2,128)S(1)}, f32[2,256,64]{1,2,0:T(8,128)S(1)}, f32[2,64]{1,0:T(2,128)S(1)}, /...) while((s32[]{:T(128)}, f32[2,64,256]{2,1,0:T(8,128)S(1)}, ...), condition=%wide.region_17.18_spmd, body=%wide.region_12.17_spmd.sunk | while | flops 127755136 | bytes 2386049 | solution.py:90
  164.9 11.2 %collective-permute-done.2 = f32[2,33088]{1,0:T(2,128)S(1)} collective-permute-done((f32[2,33088]{1,0:T(2,128)S(1)}, f32[2,33088]{1,0:T(2,128)S(1)}, u32[]{:S(2)}, u32[]{:S(2)}) %collective-permute-start.2) | collective-permute-done | bytes 264736 | tf_op jit(solution)/shard_map/state_hop/ppermute | solution.py:16
  176.5 10.8 %while.133 = (s32[]{:T(128)}, f32[2,64,256]{2,1,0:T(8,128)S(1)}, f32[2,256]{1,0:T(2,128)S(1)}, f32[2,256,64]{1,2,0:T(8,128)S(1)}, f32[2,64]{1,0:T(2,128)S(1)}, /...) while((s32[]{:T(128)}, f32[2,64,256]{2,1,0:T(8,128)S(1)}, ...), condition=%wide.region_23.24_spmd, body=%wide.region_18.23_spmd.sunk | while | flops 127755136 | bytes 2386049 | solution.py:90
  189.8 10.4 %collective-permute-done.3 = f32[2,33088]{1,0:T(2,128)S(1)} collective-permute-done((f32[2,33088]{1,0:T(2,128)S(1)}, f32[2,33088]{1,0:T(2,128)S(1)}, u32[]{:S(2)}, u32[]{:S(2)}) %collective-permute-start.3) | collective-permute-done | bytes 264736 | tf_op jit(solution)/shard_map/state_hop/ppermute | solution.py:16
  200.6 10.8 %while.134 = (s32[]{:T(128)}, f32[2,64,256]{2,1,0:T(8,128)S(1)}, f32[2,256]{1,0:T(2,128)S(1)}, f32[2,256,64]{1,2,0:T(8,128)S(1)}, f32[2,64]{1,0:T(2,128)S(1)}, /...) while((s32[]{:T(128)}, f32[2,64,256]{2,1,0:T(8,128)S(1)}, ...), condition=%wide.region_29.30_spmd, body=%wide.region_24.29_spmd.sunk | while | flops 127755136 | bytes 2386049 | solution.py:90
  213.9 10.0 %collective-permute-done.4 = f32[2,33088]{1,0:T(2,128)S(1)} collective-permute-done((f32[2,33088]{1,0:T(2,128)S(1)}, f32[2,33088]{1,0:T(2,128)S(1)}, u32[]{:S(2)}, u32[]{:S(2)}) %collective-permute-start.4) | collective-permute-done | bytes 264736 | tf_op jit(solution)/shard_map/state_hop/ppermute | solution.py:16
  224.3 10.8 %while.135 = (s32[]{:T(128)}, f32[2,64,256]{2,1,0:T(8,128)S(1)}, f32[2,256]{1,0:T(2,128)S(1)}, f32[2,256,64]{1,2,0:T(8,128)S(1)}, f32[2,64]{1,0:T(2,128)S(1)}, /...) while((s32[]{:T(128)}, f32[2,64,256]{2,1,0:T(8,128)S(1)}, ...), condition=%wide.region_35.36_spmd, body=%wide.region_30.35_spmd.sunk | while | flops 127755136 | bytes 2386049 | solution.py:90
  237.6 10.0 %collective-permute-done.5 = f32[2,33088]{1,0:T(2,128)S(1)} collective-permute-done((f32[2,33088]{1,0:T(2,128)S(1)}, f32[2,33088]{1,0:T(2,128)S(1)}, u32[]{:S(2)}, u32[]{:S(2)}) %collective-permute-start.5) | collective-permute-done | bytes 264736 | tf_op jit(solution)/shard_map/state_hop/ppermute | solution.py:16
  248.0 10.8 %while.136 = (s32[]{:T(128)}, f32[2,64,256]{2,1,0:T(8,128)S(1)}, f32[2,256]{1,0:T(2,128)S(1)}, f32[2,256,64]{1,2,0:T(8,128)S(1)}, f32[2,64]{1,0:T(2,128)S(1)}, /...) while((s32[]{:T(128)}, f32[2,64,256]{2,1,0:T(8,128)S(1)}, ...), condition=%wide.region_41.42_spmd, body=%wide.region_36.41_spmd.sunk | while | flops 127755136 | bytes 2386049 | solution.py:90
  259.3 2.1 collective-permute-start.6
  261.8 9.4 %collective-permute-done.6 = f32[2,33088]{1,0:T(2,128)S(1)} collective-permute-done((f32[2,33088]{1,0:T(2,128)S(1)}, f32[2,33088]{1,0:T(2,128)S(1)}, u32[]{:S(2)}, u32[]{:S(2)}) %collective-permute-start.6) | collective-permute-done | bytes 264736 | tf_op jit(solution)/shard_map/state_hop/ppermute | solution.py:16
  271.7 20.8 %while.137 = (s32[]{:T(128)}, f32[2,64,256]{2,1,0:T(8,128)S(1)}, f32[2,256]{1,0:T(2,128)S(1)}, f32[2,256,64]{1,2,0:T(8,128)S(1)}, f32[2,64]{1,0:T(2,128)S(1)}, /...) while((s32[]{:T(128)}, f32[2,64,256]{2,1,0:T(8,128)S(1)}, ...), condition=%wide.region_49.50_spmd, body=%wide.region_42.49_spmd.sunk | while | flops 273236992 | bytes 4856473 | solution.py:90
  292.6 6.5 %all_to_all.15 = bf16[4,2,4096]{2,1,0:T(2,128)(2,1)S(1)} all-to-all(bf16[4,2,4096]{2,1,0:T(2,128)(2,1)S(1)} %reshape.535), channel_id=1, replica_groups=mesh['seq'=8,'xlo'=2,'z'=8,'core'=2] {'xlo','core'}, dimensions={0} | all-to-all | bytes 131072 | tf_op jit(solution)/shard_map/output_mix/all_to_all | solution.py:182
  301.3 46.7 %all_to_all.16 = f32[8,2,8,3072]{3,2,1,0:T(8,128)S(1)} all-to-all(f32[8,2,8,3072]{3,2,1,0:T(8,128)S(1)} %copy.215), channel_id=1, replica_groups=mesh['seq'=8,'xlo'=2,'z'=8,'core'=2] {'z'}, dimensions={0} | all-to-all | bytes 3145728 | tf_op jit(solution)/shard_map/output_mix/all_to_all | solution.py:189
  (688 shorter events, 114.6 us)
Async XLA Ops:
  9.5 82.3 %all-to-all-start = ((bf16[32,2,8,3072]{3,2,1,0:T(8,128)(2,1)}), bf16[32,2,8,3072]{3,2,1,0:T(8,128)(2,1)S(1)}, u32[]{:S(2)}, u32[]{:S(2)}) async-start(bf16[32,2,8,3072]{3,2,1,0:T(8,128)(2,1)} %stack.2), calls=%async_computation | async-start | bytes 6291456 | tf_op jit(solution)/shard_map/all_to_all | solution.py:133
  19.0 117.5 %all-gather.2.cloned.1.call-start = ((), (), s32[]{:S(2)}) async-start(), calls=%async_computation.3 | async-start | bytes 1966080 | tf_op jit(solution)/shard_map/all_gather | solution.py:143
  19.7 72.3 %copy-start.7 = (bf16[1,3072]{1,0:T(2,128)(2,1)S(1)}, bf16[1,3072]{1,0:T(2,128)(2,1)}, u32[]{:S(2)}) copy-start(bf16[1,3072]{1,0:T(2,128)(2,1)} %param.29) | copy-start | bytes 18436
  91.8 1.3 copy-start.6
  94.2 0.9 copy-start
  94.2 0.9 copy-start.4
  94.2 0.9 copy-start.5
  94.2 0.9 copy-start.3
  94.3 0.9 copy-start.1
  94.3 0.9 copy-start.2
  106.5 13.4 %collective-permute-start = (f32[2,33088]{1,0:T(2,128)S(1)}, f32[2,33088]{1,0:T(2,128)S(1)}, u32[]{:S(2)}, u32[]{:S(2)}) collective-permute-start(f32[2,33088]{1,0:T(2,128)S(1)} %pad_maximum_fusion), channel_id=1, source_target_pairs={{0,32},{32,64},{64,96},{96,128},{128,160},{160,192},{192,224},{1,3... | collective-permute-start | bytes 794120 | tf_op jit(solution)/shard_map/state_hop/ppermute | solution.py:16
  137.0 14.1 %collective-permute-start.1 = (f32[2,33088]{1,0:T(2,128)S(1)}, f32[2,33088]{1,0:T(2,128)S(1)}, u32[]{:S(2)}, u32[]{:S(2)}) collective-permute-start(f32[2,33088]{1,0:T(2,128)S(1)} %pad_maximum_fusion.1), channel_id=1, source_target_pairs={{0,32},{32,64},{64,96},{96,128},{128,160},{160,192},{192,224},{1,3... | collective-permute-start | bytes 794120 | tf_op jit(solution)/shard_map/state_hop/ppermute | solution.py:16
  162.8 13.3 %collective-permute-start.2 = (f32[2,33088]{1,0:T(2,128)S(1)}, f32[2,33088]{1,0:T(2,128)S(1)}, u32[]{:S(2)}, u32[]{:S(2)}) collective-permute-start(f32[2,33088]{1,0:T(2,128)S(1)} %pad_maximum_fusion.2), channel_id=1, source_target_pairs={{0,32},{32,64},{64,96},{96,128},{128,160},{160,192},{192,224},{1,3... | collective-permute-start | bytes 794120 | tf_op jit(solution)/shard_map/state_hop/ppermute | solution.py:16
  187.9 12.4 %collective-permute-start.3 = (f32[2,33088]{1,0:T(2,128)S(1)}, f32[2,33088]{1,0:T(2,128)S(1)}, u32[]{:S(2)}, u32[]{:S(2)}) collective-permute-start(f32[2,33088]{1,0:T(2,128)S(1)} %pad_maximum_fusion.3), channel_id=1, source_target_pairs={{0,32},{32,64},{64,96},{96,128},{128,160},{160,192},{192,224},{1,3... | collective-permute-start | bytes 794120 | tf_op jit(solution)/shard_map/state_hop/ppermute | solution.py:16
  212.0 11.9 %collective-permute-start.4 = (f32[2,33088]{1,0:T(2,128)S(1)}, f32[2,33088]{1,0:T(2,128)S(1)}, u32[]{:S(2)}, u32[]{:S(2)}) collective-permute-start(f32[2,33088]{1,0:T(2,128)S(1)} %pad_maximum_fusion.4), channel_id=1, source_target_pairs={{0,32},{32,64},{64,96},{96,128},{128,160},{160,192},{192,224},{1,3... | collective-permute-start | bytes 794120 | tf_op jit(solution)/shard_map/state_hop/ppermute | solution.py:16
  235.7 11.9 %collective-permute-start.5 = (f32[2,33088]{1,0:T(2,128)S(1)}, f32[2,33088]{1,0:T(2,128)S(1)}, u32[]{:S(2)}, u32[]{:S(2)}) collective-permute-start(f32[2,33088]{1,0:T(2,128)S(1)} %pad_maximum_fusion.5), channel_id=1, source_target_pairs={{0,32},{32,64},{64,96},{96,128},{128,160},{160,192},{192,224},{1,3... | collective-permute-start | bytes 794120 | tf_op jit(solution)/shard_map/state_hop/ppermute | solution.py:16
  259.3 11.9 %collective-permute-start.6 = (f32[2,33088]{1,0:T(2,128)S(1)}, f32[2,33088]{1,0:T(2,128)S(1)}, u32[]{:S(2)}, u32[]{:S(2)}) collective-permute-start(f32[2,33088]{1,0:T(2,128)S(1)} %pad_maximum_fusion.6), channel_id=1, source_target_pairs={{0,32},{32,64},{64,96},{96,128},{128,160},{160,192},{192,224},{1,3... | collective-permute-start | bytes 794120 | tf_op jit(solution)/shard_map/state_hop/ppermute | solution.py:16
Sparse Core Ops, SparseCore 0:
  110.3 26.1 all-gather.1
